TPU v7x, 128 devices: a whole 4x4x4 slice. The times are simulated.
128 devices in a mesh: row: 8 (over y_hi, x), col: 16 (over y_lo, z, core).
Axes of the slice: x: 4, y: 4 (y_hi: 2, y_lo: 2; y = y_hi * 2 + y_lo), z: 4, core: 2. Of those that a mesh axis runs over, the one named last changes fastest.
Arguments:
- samples: bfloat16 [1024, 200192], P(('row', 'col')), may hold values from -6 to 6
- pfb_taps: float32 [8, 512], replicated, may hold values from -2 to 2
- antenna_input_row: int32 [1024], replicated, may hold values from 0 to 1023, each once
- positions: float32 [2, 1024], P(None, ('row', 'col')), may hold values from -300 to 300
- directions: float32 [2, 1024], replicated, may hold values from -0.05 to 0.05
- pointing: int32 [1024], replicated, may hold values from 0 to 1023, each once
Outputs:
- visibilities: float32 [256, 2, 1024, 1024], P(('row', 'col'))
- beam_power: float32 [256, 24, 1024], P(('row', 'col'))
Inputs may be any that keep to these rules, and one draw needn't show every extreme that they name: A permutation: antenna a's samples arrive in input row antenna_input_row[a]. A permutation: beam b points to table row pointing[b], each row used by exactly one beam.
All inputs are finite; a program needn't handle non-finite values.
Results may differ from a plain program's by a relative error of at most 0.0034.
Values may be sent and summed in bfloat16 or wider, within the bound.
A program may use at most 128 MiB of HBM per device.

v0:
```python
import functools
import math

import jax
import jax.numpy as jnp
import ml_dtypes
import numpy as np
from jax import lax
from jax.experimental import pallas as pl
from jax.experimental.pallas import tpu as pltpu
from jax.sharding import PartitionSpec as P

MESH = pl.DeviceIdType.MESH
ROWS, COLS = 8, 16
DEVICES = ROWS * COLS
ANT = 1024
BEAMS = 1024
LOCAL = 8
FRAME = 512
HALF = 256
TAPS = 8
CHUNKS = 3
SPC = 128
SPECTRA = CHUNKS * SPC
INTEG = 16
CHANNELS = 256
NT = (((1,), (1,)), ((), ()))
NN = (((1,), (0,)), ((), ()))
F32, BF16 = jnp.float32, jnp.bfloat16


def dft_tables():
    n = np.arange(HALF)
    d = np.arange(CHANNELS // 2)
    tables = []
    for parity in range(2):
        angle = 2.0 * np.pi * ((2 * d[:, None] + parity) * n[None, :] % FRAME) / FRAME
        tables.append(np.concatenate([np.cos(angle), -np.sin(angle)], 0) / math.sqrt(FRAME))
    table = np.stack(tables)
    high = table.astype(ml_dtypes.bfloat16)
    low = (table - high.astype(np.float64)).astype(ml_dtypes.bfloat16)
    return high, low


def sine_coefficients():
    theta = (np.arange(4000) + 0.5) * np.pi / 8000
    w = 0.25 * np.cos(theta)
    basis = np.stack([w ** (2 * j + 1) for j in range(6)], 1)
    return np.linalg.lstsq(basis, np.sin(2 * np.pi * w), rcond=None)[0]


SINE = [float(v) / math.sqrt(ANT) for v in sine_coefficients()]


def sine(w):
    z = w * w
    acc = SINE[-1] * z + SINE[-2]
    for coefficient in SINE[-3::-1]:
        acc = acc * z + coefficient
    return acc * w


def column(row):
    return jnp.transpose(jnp.broadcast_to(row.astype(F32), (128, 128)))


def main_kernel(samples, taps, thigh, tlow, antrow, pos, dirs, pointing,
                xs, beam,
                eo, stage, send, recv, pos1, pos2, table, weights, perm, lcol, mcol, plain, full,
                lsem, ssem, rsem, psem, qsem):
    r, c = lax.axis_index("row"), lax.axis_index("col")
    me = r * COLS + c
    cts = [lax.rem(c + k, COLS) for k in range(COLS)]

    def each(fn):
        def outer(j, carry):
            for k in range(COLS):
                rt = lax.rem(r + j + (3 * k) % ROWS, ROWS)
                if k == 0:
                    @pl.when(j > 0)
                    def _():
                        fn(rt, cts[0])
                else:
                    fn(rt, cts[k])
            return carry
        lax.fori_loop(0, ROWS, outer, 0)

    barrier = pltpu.get_barrier_semaphore()
    each(lambda rt, ct: pl.semaphore_signal(barrier, inc=1, device_id=(rt, ct), device_id_type=MESH))

    def channelize(chunk):
        def filt(u, carry):
            first = chunk * SPC + 8 * u
            for j in range(2):
                halves = []
                for lane in (j * 128, j * 128 + HALF):
                    frames = [
                        samples[:, pl.ds(pl.multiple_of((first + f) * FRAME + lane, 128), 128)].astype(F32)
                        for f in range(8 + TAPS - 1)
                    ]
                    tap = [jnp.broadcast_to(taps[t:t + 1, lane:lane + 128], (8, 128)) for t in range(TAPS)]
                    sums = []
                    for s in range(8):
                        acc = tap[0] * frames[s]
                        for t in range(1, TAPS):
                            acc = acc + tap[t] * frames[s + t]
                        sums.append(acc)
                    halves.append(sums)
                for s in range(8):
                    at = pl.ds(8 * u + s, 8, stride=SPC)
                    eo[j, at, :] = halves[0][s] + halves[1][s]
                    eo[2 + j, at, :] = halves[0][s] - halves[1][s]
            return carry
        lax.fori_loop(0, SPC // 8, filt, 0)

        def dft(g, carry):
            for p in range(2):
                rows = pl.ds(pl.multiple_of(g * 256, 256), 256)
                x = jnp.concatenate([eo[2 * p, rows, :], eo[2 * p + 1, rows, :]], 1)
                hi = x.astype(BF16)
                lo = (x - hi.astype(F32)).astype(BF16)
                res = lax.dot_general(thigh[p], hi, NT, preferred_element_type=F32)
                res = res + lax.dot_general(thigh[p], lo, NT, preferred_element_type=F32)
                res = res + lax.dot_general(tlow[p], hi, NT, preferred_element_type=F32)
                for q in range(2):
                    for i in range(2):
                        stage[pl.ds(p * 16 + q * 8 + i + 2 * g, 128, stride=32), :] = (
                            res[q * 128:(q + 1) * 128, i * 128:(i + 1) * 128])
            return carry
        lax.fori_loop(0, LOCAL // 2, dft, 0)

        def pack(u, carry):
            block = stage[pl.ds(pl.multiple_of(u * 256, 256), 256), :]
            send[chunk, pl.ds(u * 8, 8)] = block.reshape(8, 32, 128).astype(BF16)
            return carry
        lax.fori_loop(0, 16, pack, 0)

    def launch(chunk):
        each(lambda rt, ct: pltpu.make_async_remote_copy(
            src_ref=send.at[chunk, rt * COLS + ct], dst_ref=recv.at[chunk, me],
            send_sem=ssem.at[chunk], recv_sem=rsem.at[chunk],
            device_id=(rt, ct), device_id_type=MESH).start())
        pltpu.make_async_copy(send.at[chunk, me], recv.at[chunk, me], lsem.at[chunk]).start()

    channelize(0)
    pl.semaphore_wait(barrier, DEVICES - 1)
    launch(0)
    pltpu.make_async_copy(pos, pos1.at[r], lsem.at[3]).start()
    for j in range(1, ROWS):
        pltpu.make_async_remote_copy(
            src_ref=pos, dst_ref=pos1.at[r], send_sem=psem.at[0], recv_sem=psem.at[1],
            device_id=(lax.rem(r + j, ROWS), c), device_id_type=MESH).start()
    channelize(1)
    launch(1)
    pltpu.make_async_copy(pos, pos1.at[r], lsem.at[3]).wait()
    pltpu.make_async_copy(pos1.at[pl.ds(0, ROWS - 1)], pos1.at[pl.ds(0, ROWS - 1)], psem.at[0]).wait()
    pltpu.make_async_copy(pos1.at[pl.ds(0, ROWS - 1)], pos1.at[pl.ds(0, ROWS - 1)], psem.at[1]).wait()
    pltpu.make_async_copy(pos1, pos2.at[c], lsem.at[3]).start()
    for k in range(1, COLS):
        pltpu.make_async_remote_copy(
            src_ref=pos1, dst_ref=pos2.at[c], send_sem=qsem.at[0], recv_sem=qsem.at[1],
            device_id=(r, cts[k]), device_id_type=MESH).start()
    channelize(2)
    launch(2)

    lane = lax.broadcasted_iota(jnp.int32, (128, 128), 1).astype(F32)
    for blk in range(8):
        wanted = column(antrow[blk:blk + 1, :])
        for t in range(8):
            perm[blk * 128:(blk + 1) * 128, t * 128:(t + 1) * 128] = (
                jnp.where(wanted == lane + 128.0 * t, 1.0, 0.0).astype(BF16))
        wanted = column(pointing[blk:blk + 1, :])
        l_sum = jnp.zeros((128, 128), F32)
        m_sum = jnp.zeros((128, 128), F32)
        for t in range(8):
            hit = wanted == lane + 128.0 * t
            l_sum = l_sum + jnp.where(hit, dirs[0:1, t * 128:(t + 1) * 128], 0.0)
            m_sum = m_sum + jnp.where(hit, dirs[1:2, t * 128:(t + 1) * 128], 0.0)
        lcol[blk * 128:(blk + 1) * 128, :] = jnp.broadcast_to(jnp.sum(l_sum, 1, keepdims=True), (128, 128))
        mcol[blk * 128:(blk + 1) * 128, :] = jnp.broadcast_to(jnp.sum(m_sum, 1, keepdims=True), (128, 128))

    pltpu.make_async_copy(pos1, pos2.at[c], lsem.at[3]).wait()
    for s in range(2):
        pltpu.make_async_copy(pos2.at[pl.ds(0, COLS - 1)], pos2.at[pl.ds(0, COLS - 1)], qsem.at[s]).wait()

    def spread(i, carry):
        table[pl.ds(i, 1), :] = pos2[i // ROWS, i % ROWS]
        return carry
    lax.fori_loop(0, DEVICES, spread, 0)
    rest = table[...]
    parts = []
    for _ in range(3):
        part = rest.astype(BF16)
        rest = rest - part.astype(F32)
        parts.append(part)
    picked = []
    antenna = lax.broadcasted_iota(jnp.int32, (128, ANT), 1)
    entry = lax.broadcasted_iota(jnp.int32, (128, ANT), 0)
    mine = (entry % ROWS) * COLS + entry // ROWS == antenna // LOCAL
    for xy in range(2):
        pick = jnp.where(entry == antenna % LOCAL + LOCAL * xy, 1.0, 0.0).astype(BF16)
        whole = sum(lax.dot_general(part, pick, NN, preferred_element_type=F32) for part in parts[::-1])
        picked.append(jnp.sum(jnp.where(mine, whole, 0.0), 0, keepdims=True))
    xpos, ypos = picked

    factors = [(2 * me + p + 1).astype(F32) * (1.0 / CHANNELS) for p in range(2)]

    def weigh(u, carry):
        rows = pl.ds(pl.multiple_of(u * 16, 16), 16)
        l_here, m_here = lcol[rows, :], mcol[rows, :]
        for t in range(8):
            cols = slice(t * 128, (t + 1) * 128)
            delay = l_here * xpos[:, cols] + m_here * ypos[:, cols]
            for p in range(2):
                turns = delay * factors[p]
                turns = turns - jnp.round(turns)
                weights[p, rows, t * 128:(t + 1) * 128] = sine(0.25 - jnp.abs(turns)).astype(BF16)
                w = 0.25 - jnp.abs(0.25 - turns)
                weights[p, rows, ANT + t * 128:ANT + (t + 1) * 128] = sine(jnp.maximum(w, -0.5 - w)).astype(BF16)
        return carry
    lax.fori_loop(0, BEAMS // 16, weigh, 0)

    for chunk in range(CHUNKS):
        pltpu.make_async_copy(send.at[chunk, me], recv.at[chunk, me], lsem.at[chunk]).wait()
        every = pl.ds(0, DEVICES - 1)
        pltpu.make_async_copy(send.at[chunk, every], recv.at[chunk, every], rsem.at[chunk]).wait()
        for p in range(2):
            def gather(u, carry):
                z = recv[chunk, pl.ds(u * 16, 16), p * 16:(p + 1) * 16, :].astype(F32)
                rows = pl.ds(pl.multiple_of(u * 128, 128), 128)
                plain[rows, 0:128] = z[:, 0:8, :].reshape(128, 128).astype(BF16)
                plain[rows, 128:256] = z[:, 8:16, :].reshape(128, 128).astype(BF16)
                return carry
            lax.fori_loop(0, 8, gather, 0)

            def order(u, carry):
                rows = pl.ds(pl.multiple_of(u * 256, 256), 256)
                x = lax.dot_general(perm[rows, :], plain[...], NN, preferred_element_type=F32)
                xb = x.astype(BF16)
                full[rows, :] = xb
                xs[p, rows, chunk * 256:(chunk + 1) * 256] = xb
                below = pl.ds(pl.multiple_of(ANT + u * 256, 256), 256)
                full[below, 0:128] = x[:, 128:256].astype(BF16)
                full[below, 128:256] = (-x[:, 0:128]).astype(BF16)
                return carry
            lax.fori_loop(0, 4, order, 0)

            def form(u, carry):
                rows = pl.ds(pl.multiple_of(u * 256, 256), 256)
                v = lax.dot_general(weights[p, rows, :], full[...], NN, preferred_element_type=F32)
                power = v[:, 0:128] * v[:, 0:128] + v[:, 128:256] * v[:, 128:256]
                bins = jnp.sum(jnp.transpose(power).reshape(SPC // INTEG, INTEG, 256), axis=1)
                beam[p, chunk * 8:(chunk + 1) * 8, pl.ds(pl.multiple_of(u * 256, 256), 256)] = bins
                return carry
            lax.fori_loop(0, 4, form, 0)

    for chunk in range(CHUNKS):
        every = pl.ds(0, DEVICES - 1)
        pltpu.make_async_copy(send.at[chunk, every], recv.at[chunk, every], ssem.at[chunk]).wait()


def gram_kernel(x, out):
    u = pl.program_id(1)
    left = x[0, pl.ds(pl.multiple_of(u * 256, 256), 256), :]
    scale = 1.0 / SPECTRA
    out[0, 0] = lax.dot_general(left, x[0], NT, preferred_element_type=F32) * scale
    turned = jnp.concatenate(
        [piece for k in range(CHUNKS) for piece in (left[:, k * 256 + 128:(k + 1) * 256], -left[:, k * 256:k * 256 + 128])], 1)
    out[0, 1] = lax.dot_general(turned, x[0], NT, preferred_element_type=F32) * scale


def body(samples, pfb_taps, antenna_input_row, positions, directions, pointing):
    high, low = dft_tables()
    pos = jnp.pad(positions.reshape(1, 2 * LOCAL), ((0, 0), (0, 128 - 2 * LOCAL)))
    vmem = pl.BlockSpec(memory_space=pltpu.VMEM)
    xs, beam = pl.pallas_call(
        main_kernel,
        out_shape=(jax.ShapeDtypeStruct((2, ANT, 2 * SPECTRA), BF16),
                   jax.ShapeDtypeStruct((2, SPECTRA // INTEG, BEAMS), F32)),
        in_specs=[vmem] * 8,
        out_specs=(vmem, vmem),
        scratch_shapes=[
            pltpu.VMEM((4, LOCAL * SPC, 128), F32),
            pltpu.VMEM((DEVICES * 32, 128), F32),
            pltpu.VMEM((CHUNKS, DEVICES, 32, 128), BF16),
            pltpu.VMEM((CHUNKS, DEVICES, 32, 128), BF16),
            pltpu.VMEM((ROWS, 1, 128), F32),
            pltpu.VMEM((COLS, ROWS, 1, 128), F32),
            pltpu.VMEM((DEVICES, 128), F32),
            pltpu.VMEM((2, BEAMS, 2 * ANT), BF16),
            pltpu.VMEM((ANT, ANT), BF16),
            pltpu.VMEM((BEAMS, 128), F32),
            pltpu.VMEM((BEAMS, 128), F32),
            pltpu.VMEM((ANT, 256), BF16),
            pltpu.VMEM((2 * ANT, 256), BF16),
            pltpu.SemaphoreType.DMA((4,)),
            pltpu.SemaphoreType.DMA((CHUNKS,)),
            pltpu.SemaphoreType.DMA((CHUNKS,)),
            pltpu.SemaphoreType.DMA((2,)),
            pltpu.SemaphoreType.DMA((2,)),
        ],
        compiler_params=pltpu.CompilerParams(
            collective_id=0, has_side_effects=True, vmem_limit_bytes=60 * 1024 * 1024),
        name="channelize_exchange_beams",
    )(samples, pfb_taps, jnp.asarray(high), jnp.asarray(low), antenna_input_row.reshape(8, 128), pos,
      directions, pointing.reshape(8, 128))
    vis = pl.pallas_call(
        gram_kernel,
        grid=(2, 4),
        out_shape=jax.ShapeDtypeStruct((2, 2, ANT, ANT), F32),
        in_specs=[pl.BlockSpec((1, ANT, 2 * SPECTRA), lambda p, u: (p, 0, 0))],
        out_specs=pl.BlockSpec((1, 2, 256, ANT), lambda p, u: (p, 0, u, 0)),
        compiler_params=pltpu.CompilerParams(vmem_limit_bytes=40 * 1024 * 1024),
        name="visibilities",
    )(xs)
    return vis, beam


def solution(mesh):
    return jax.shard_map(
        body,
        mesh=mesh,
        in_specs=(P(("row", "col"), None), P(), P(), P(None, ("row", "col")), P(), P()),
        out_specs=(P(("row", "col"), None, None, None), P(("row", "col"), None, None)),
        check_vma=False,
    )
```

profile of v0, /device:TPU:19, one launch (start us, length us, event | category | flops | bytes accessed | tf_op | source)
XLA Modules:
  0.0 94.7 jit_solution(5570256476726712880)
XLA Ops:
  0.6 0.8 reshape.14
  1.4 0.5 pad.4.pos
  1.9 79.9 %channelize_exchange_beams.1 = (bf16[2,1024,768]{2,1,0:T(8,128)(2,1)}, f32[2,24,1024]{2,1,0:T(8,128)}) custom-call(bf16[8,200192]{1,0:T(8,128)(2,1)} %samples.1, f32[8,512]{1,0:T(8,128)} %taps.1, bf16[2,256,256]{2,1,0:T(8,128)(2,1)} %constant.7.clone.thigh, bf16[2,256,256]{2,1,0:T(8,128)(2,1)} %constant.8.clone.tlow, s32[8,128]{1,0:T(8,128)} %bitcast.2, ...), custom_call_target="tpu_custom_call" | custom-call | tf_op jit(solution)/shard_map/channelize_exchange_beams/pallas_call | solution.py:276
  81.8 0.0 copy-start
  81.8 1.9 %copy-done = bf16[2,1024,768]{2,1,0:T(8,128)(2,1)S(1)} copy-done((bf16[2,1024,768]{2,1,0:T(8,128)(2,1)S(1)}, bf16[2,1024,768]{2,1,0:T(8,128)(2,1)}, u32[]{:S(2)}) %copy-start) | copy-done | bytes 3145752
  83.7 0.0 copy-start.1
  83.7 10.3 %visibilities.1 = f32[2,2,1024,1024]{3,2,1,0:T(8,128)} custom-call(bf16[2,1024,768]{2,1,0:T(8,128)(2,1)S(1)} %copy-done), custom_call_target="tpu_custom_call" | custom-call | tf_op jit(solution)/shard_map/visibilities/pallas_call | solution.py:307
  94.1 0.0 copy-done.1
  94.1 0.7 copy.11
Async XLA Ops:
  81.8 1.9 %copy-start = (bf16[2,1024,768]{2,1,0:T(8,128)(2,1)S(1)}, bf16[2,1024,768]{2,1,0:T(8,128)(2,1)}, u32[]{:S(2)}) copy-start(bf16[2,1024,768]{2,1,0:T(8,128)(2,1)} %get-tuple-element.4.x) | copy-start | bytes 9437188
  83.7 10.4 %copy-start.1 = (f32[2,24,1024]{2,1,0:T(8,128)S(1)}, f32[2,24,1024]{2,1,0:T(8,128)}, u32[]{:S(2)}) copy-start(f32[2,24,1024]{2,1,0:T(8,128)} %get-tuple-element.9) | copy-start | bytes 589828
where the time goes:
time: 94.9 us; the launch traced here: 94.7 us
  Pallas kernels  90.3 us (95%)
  local copies, waits for them, and re-layouts  3.84 us (4%)
    pallas_call x1, Pallas kernels, body(): pl.pallas_call(main_kernel, out_shape=(jax.ShapeDtypeStruct((2, ANT, 2 *...  79.9 us
    pallas_call x1, Pallas kernels, body(): pl.pallas_call(gram_kernel, grid=(2, 4), out_shape=jax.ShapeDtypeStruct((...  10.3 us
    unnamed x5, local copies, waits for them, and re-layouts  2.56 us

commit v1 on v0

--- a/solution.py
+++ b/solution.py
@@ -23,6 +23,8 @@
 SPC = 128
 SPECTRA = CHUNKS * SPC
 INTEG = 16
+PITCH = SPC + 1
+BLOCK = 33
 CHANNELS = 256
 NT = (((1,), (1,)), ((), ()))
 NN = (((1,), (0,)), ((), ()))
@@ -45,7 +47,7 @@
 def sine_coefficients():
     theta = (np.arange(4000) + 0.5) * np.pi / 8000
     w = 0.25 * np.cos(theta)
-    basis = np.stack([w ** (2 * j + 1) for j in range(6)], 1)
+    basis = np.stack([w ** (2 * j + 1) for j in range(5)], 1)
     return np.linalg.lstsq(basis, np.sin(2 * np.pi * w), rcond=None)[0]
 
 
@@ -70,23 +72,27 @@
                 lsem, ssem, rsem, psem, qsem):
     r, c = lax.axis_index("row"), lax.axis_index("col")
     me = r * COLS + c
-    cts = [lax.rem(c + k, COLS) for k in range(COLS)]
-
-    def each(fn):
-        def outer(j, carry):
-            for k in range(COLS):
-                rt = lax.rem(r + j + (3 * k) % ROWS, ROWS)
-                if k == 0:
-                    @pl.when(j > 0)
-                    def _():
-                        fn(rt, cts[0])
-                else:
-                    fn(rt, cts[k])
-            return carry
-        lax.fori_loop(0, ROWS, outer, 0)
+
+    def peer(i):
+        k, j = lax.rem(i, COLS), lax.div(i, COLS)
+        return lax.rem(r + j + 3 * k, ROWS), lax.rem(c + k, COLS)
 
     barrier = pltpu.get_barrier_semaphore()
-    each(lambda rt, ct: pl.semaphore_signal(barrier, inc=1, device_id=(rt, ct), device_id_type=MESH))
+
+    def greet(first, count):
+        for v in range(count):
+            pl.semaphore_signal(barrier, inc=1, device_id=peer(first + v), device_id_type=MESH)
+
+    def launch(chunk, first, count):
+        for v in range(count):
+            rt, ct = peer(first + v)
+            pltpu.make_async_remote_copy(
+                src_ref=send.at[chunk, rt * COLS + ct], dst_ref=recv.at[chunk, me],
+                send_sem=ssem.at[chunk], recv_sem=rsem.at[chunk],
+                device_id=(rt, ct), device_id_type=MESH).start()
+
+    def own(chunk):
+        return pltpu.make_async_copy(send.at[chunk, me], recv.at[chunk, me], lsem.at[chunk])
 
     def channelize(chunk):
         def filt(u, carry):
@@ -107,16 +113,28 @@
                         sums.append(acc)
                     halves.append(sums)
                 for s in range(8):
-                    at = pl.ds(8 * u + s, 8, stride=SPC)
+                    at = pl.ds(8 * u + s, 8, stride=PITCH)
                     eo[j, at, :] = halves[0][s] + halves[1][s]
                     eo[2 + j, at, :] = halves[0][s] - halves[1][s]
+            if chunk > 0:
+                launch(chunk - 1, 1 + 5 * u, 5)
             return carry
-        lax.fori_loop(0, SPC // 8, filt, 0)
+
+        if chunk == 0:
+            def greeting(u, carry):
+                greet(1 + 8 * u, 8)
+                return filt(u, carry)
+            lax.fori_loop(0, SPC // 8 - 1, greeting, 0)
+            greet(DEVICES - 7, 7)
+            filt(SPC // 8 - 1, 0)
+        else:
+            lax.fori_loop(0, SPC // 8, filt, 0)
 
         def dft(g, carry):
             for p in range(2):
-                rows = pl.ds(pl.multiple_of(g * 256, 256), 256)
-                x = jnp.concatenate([eo[2 * p, rows, :], eo[2 * p + 1, rows, :]], 1)
+                x = jnp.concatenate([
+                    jnp.concatenate([eo[2 * p + j, pl.ds((2 * g + i) * PITCH, SPC), :] for j in range(2)], 1)
+                    for i in range(2)], 0)
                 hi = x.astype(BF16)
                 lo = (x - hi.astype(F32)).astype(BF16)
                 res = lax.dot_general(thigh[p], hi, NT, preferred_element_type=F32)
@@ -124,34 +142,36 @@
                 res = res + lax.dot_general(tlow[p], hi, NT, preferred_element_type=F32)
                 for q in range(2):
                     for i in range(2):
-                        stage[pl.ds(p * 16 + q * 8 + i + 2 * g, 128, stride=32), :] = (
+                        stage[pl.ds(p * 16 + q * 8 + i + 2 * g, 128, stride=BLOCK), :] = (
                             res[q * 128:(q + 1) * 128, i * 128:(i + 1) * 128])
+            if chunk > 0:
+                launch(chunk - 1, 81 + 8 * g, 8)
             return carry
         lax.fori_loop(0, LOCAL // 2, dft, 0)
 
         def pack(u, carry):
-            block = stage[pl.ds(pl.multiple_of(u * 256, 256), 256), :]
-            send[chunk, pl.ds(u * 8, 8)] = block.reshape(8, 32, 128).astype(BF16)
+            for d in range(8):
+                block = stage[pl.ds((u * 8 + d) * BLOCK, 32), :]
+                send[chunk, u * 8 + d] = block.astype(BF16)
             return carry
-        lax.fori_loop(0, 16, pack, 0)
-
-    def launch(chunk):
-        each(lambda rt, ct: pltpu.make_async_remote_copy(
-            src_ref=send.at[chunk, rt * COLS + ct], dst_ref=recv.at[chunk, me],
-            send_sem=ssem.at[chunk], recv_sem=rsem.at[chunk],
-            device_id=(rt, ct), device_id_type=MESH).start())
-        pltpu.make_async_copy(send.at[chunk, me], recv.at[chunk, me], lsem.at[chunk]).start()
+
+        def packing(u, carry):
+            if chunk > 0:
+                launch(chunk - 1, 113 + u, 1)
+            return pack(u, carry)
+        lax.fori_loop(0, 15, packing, 0)
+        pack(15, 0)
+        if chunk > 0:
+            own(chunk - 1).start()
 
     channelize(0)
     pl.semaphore_wait(barrier, DEVICES - 1)
-    launch(0)
     pltpu.make_async_copy(pos, pos1.at[r], lsem.at[3]).start()
     for j in range(1, ROWS):
         pltpu.make_async_remote_copy(
             src_ref=pos, dst_ref=pos1.at[r], send_sem=psem.at[0], recv_sem=psem.at[1],
             device_id=(lax.rem(r + j, ROWS), c), device_id_type=MESH).start()
     channelize(1)
-    launch(1)
     pltpu.make_async_copy(pos, pos1.at[r], lsem.at[3]).wait()
     pltpu.make_async_copy(pos1.at[pl.ds(0, ROWS - 1)], pos1.at[pl.ds(0, ROWS - 1)], psem.at[0]).wait()
     pltpu.make_async_copy(pos1.at[pl.ds(0, ROWS - 1)], pos1.at[pl.ds(0, ROWS - 1)], psem.at[1]).wait()
@@ -159,9 +179,9 @@
     for k in range(1, COLS):
         pltpu.make_async_remote_copy(
             src_ref=pos1, dst_ref=pos2.at[c], send_sem=qsem.at[0], recv_sem=qsem.at[1],
-            device_id=(r, cts[k]), device_id_type=MESH).start()
+            device_id=(r, lax.rem(c + k, COLS)), device_id_type=MESH).start()
     channelize(2)
-    launch(2)
+    own(2).start()
 
     lane = lax.broadcasted_iota(jnp.int32, (128, 128), 1).astype(F32)
     for blk in range(8):
@@ -218,41 +238,41 @@
                 w = 0.25 - jnp.abs(0.25 - turns)
                 weights[p, rows, ANT + t * 128:ANT + (t + 1) * 128] = sine(jnp.maximum(w, -0.5 - w)).astype(BF16)
         return carry
-    lax.fori_loop(0, BEAMS // 16, weigh, 0)
-
-    for chunk in range(CHUNKS):
-        pltpu.make_async_copy(send.at[chunk, me], recv.at[chunk, me], lsem.at[chunk]).wait()
+
+    def weighing(u, carry):
+        launch(CHUNKS - 1, 1 + 2 * u, 2)
+        return weigh(u, carry)
+    lax.fori_loop(0, BEAMS // 16 - 1, weighing, 0)
+    launch(CHUNKS - 1, DEVICES - 1, 1)
+    weigh(BEAMS // 16 - 1, 0)
+
+    def beams(chunk, carry):
+        own(chunk).wait()
         every = pl.ds(0, DEVICES - 1)
         pltpu.make_async_copy(send.at[chunk, every], recv.at[chunk, every], rsem.at[chunk]).wait()
-        for p in range(2):
+        lanes = pl.ds(pl.multiple_of(chunk * 256, 256), 256)
+
+        def channel(p, carry):
             def gather(u, carry):
-                z = recv[chunk, pl.ds(u * 16, 16), p * 16:(p + 1) * 16, :].astype(F32)
+                z = recv[chunk, pl.ds(u * 16, 16), pl.ds(pl.multiple_of(p * 16, 16), 16), :].astype(F32)
                 rows = pl.ds(pl.multiple_of(u * 128, 128), 128)
                 plain[rows, 0:128] = z[:, 0:8, :].reshape(128, 128).astype(BF16)
                 plain[rows, 128:256] = z[:, 8:16, :].reshape(128, 128).astype(BF16)
                 return carry
             lax.fori_loop(0, 8, gather, 0)
-
-            def order(u, carry):
-                rows = pl.ds(pl.multiple_of(u * 256, 256), 256)
-                x = lax.dot_general(perm[rows, :], plain[...], NN, preferred_element_type=F32)
-                xb = x.astype(BF16)
-                full[rows, :] = xb
-                xs[p, rows, chunk * 256:(chunk + 1) * 256] = xb
-                below = pl.ds(pl.multiple_of(ANT + u * 256, 256), 256)
-                full[below, 0:128] = x[:, 128:256].astype(BF16)
-                full[below, 128:256] = (-x[:, 0:128]).astype(BF16)
-                return carry
-            lax.fori_loop(0, 4, order, 0)
-
-            def form(u, carry):
-                rows = pl.ds(pl.multiple_of(u * 256, 256), 256)
-                v = lax.dot_general(weights[p, rows, :], full[...], NN, preferred_element_type=F32)
-                power = v[:, 0:128] * v[:, 0:128] + v[:, 128:256] * v[:, 128:256]
-                bins = jnp.sum(jnp.transpose(power).reshape(SPC // INTEG, INTEG, 256), axis=1)
-                beam[p, chunk * 8:(chunk + 1) * 8, pl.ds(pl.multiple_of(u * 256, 256), 256)] = bins
-                return carry
-            lax.fori_loop(0, 4, form, 0)
+            x = lax.dot_general(perm[...], plain[...], NN, preferred_element_type=F32)
+            xb = x.astype(BF16)
+            full[0:ANT, :] = xb
+            xs[p, :, lanes] = xb
+            full[ANT:2 * ANT, 0:128] = x[:, 128:256].astype(BF16)
+            full[ANT:2 * ANT, 128:256] = (-x[:, 0:128]).astype(BF16)
+            v = lax.dot_general(weights[p], full[...], NN, preferred_element_type=F32)
+            power = v[:, 0:128] * v[:, 0:128] + v[:, 128:256] * v[:, 128:256]
+            bins = jnp.sum(jnp.transpose(power).reshape(SPC // INTEG, INTEG, BEAMS), axis=1)
+            beam[p, pl.ds(pl.multiple_of(chunk * 8, 8), 8), :] = bins
+            return carry
+        return lax.fori_loop(0, 2, channel, carry)
+    lax.fori_loop(0, CHUNKS, beams, 0)
 
     for chunk in range(CHUNKS):
         every = pl.ds(0, DEVICES - 1)
@@ -261,12 +281,12 @@
 
 def gram_kernel(x, out):
     u = pl.program_id(1)
-    left = x[0, pl.ds(pl.multiple_of(u * 256, 256), 256), :]
+    right = x[0, pl.ds(pl.multiple_of(u * 256, 256), 256), :]
     scale = 1.0 / SPECTRA
-    out[0, 0] = lax.dot_general(left, x[0], NT, preferred_element_type=F32) * scale
+    out[0, 0] = lax.dot_general(x[0], right, NT, preferred_element_type=F32) * scale
     turned = jnp.concatenate(
-        [piece for k in range(CHUNKS) for piece in (left[:, k * 256 + 128:(k + 1) * 256], -left[:, k * 256:k * 256 + 128])], 1)
-    out[0, 1] = lax.dot_general(turned, x[0], NT, preferred_element_type=F32) * scale
+        [piece for k in range(CHUNKS) for piece in (-right[:, k * 256 + 128:(k + 1) * 256], right[:, k * 256:k * 256 + 128])], 1)
+    out[0, 1] = lax.dot_general(x[0], turned, NT, preferred_element_type=F32) * scale
 
 
 def body(samples, pfb_taps, antenna_input_row, positions, directions, pointing):
@@ -280,8 +300,8 @@
         in_specs=[vmem] * 8,
         out_specs=(vmem, vmem),
         scratch_shapes=[
-            pltpu.VMEM((4, LOCAL * SPC, 128), F32),
-            pltpu.VMEM((DEVICES * 32, 128), F32),
+            pltpu.VMEM((4, LOCAL * PITCH, 128), F32),
+            pltpu.VMEM((DEVICES * BLOCK, 128), F32),
             pltpu.VMEM((CHUNKS, DEVICES, 32, 128), BF16),
             pltpu.VMEM((CHUNKS, DEVICES, 32, 128), BF16),
             pltpu.VMEM((ROWS, 1, 128), F32),
@@ -309,7 +329,7 @@
         grid=(2, 4),
         out_shape=jax.ShapeDtypeStruct((2, 2, ANT, ANT), F32),
         in_specs=[pl.BlockSpec((1, ANT, 2 * SPECTRA), lambda p, u: (p, 0, 0))],
-        out_specs=pl.BlockSpec((1, 2, 256, ANT), lambda p, u: (p, 0, u, 0)),
+        out_specs=pl.BlockSpec((1, 2, ANT, 256), lambda p, u: (p, 0, 0, u)),
         compiler_params=pltpu.CompilerParams(vmem_limit_bytes=40 * 1024 * 1024),
         name="visibilities",
     )(xs)

time: 94.9 us -> 85.2 us (0.90)
  the two profiles are of different devices: /device:TPU:19 before, /device:TPU:57 now
where the time goes in v1:
time: 85.2 us; the launch traced here: 83.8 us
  Pallas kernels  79.3 us (93%)
  local copies, waits for them, and re-layouts  3.84 us (5%)
    pallas_call x1, Pallas kernels, body(): pl.pallas_call(main_kernel, out_shape=(jax.ShapeDtypeStruct((2, ANT, 2 *...  68.9 us
    pallas_call x1, Pallas kernels, body(): pl.pallas_call(gram_kernel, grid=(2, 4), out_shape=jax.ShapeDtypeStruct((...  10.4 us
    unnamed x5, local copies, waits for them, and re-layouts  2.56 us

profile of v1, /device:TPU:57, one launch (start us, length us, event | category | flops | bytes accessed | tf_op | source)
XLA Modules:
  0.0 83.8 jit_solution(16587344284053753931)
XLA Ops:
  0.6 0.8 reshape.14
  1.4 0.5 pad.4.pos
  1.9 68.9 %channelize_exchange_beams.1 = (bf16[2,1024,768]{2,1,0:T(8,128)(2,1)}, f32[2,24,1024]{2,1,0:T(8,128)}) custom-call(bf16[8,200192]{1,0:T(8,128)(2,1)} %samples.1, f32[8,512]{1,0:T(8,128)} %taps.1, bf16[2,256,256]{2,1,0:T(8,128)(2,1)} %constant.7.clone.thigh, bf16[2,256,256]{2,1,0:T(8,128)(2,1)} %constant.8.clone.tlow, s32[8,128]{1,0:T(8,128)} %bitcast.2, ...), custom_call_target="tpu_custom_call" | custom-call | tf_op jit(solution)/shard_map/channelize_exchange_beams/pallas_call | solution.py:296
  70.9 0.0 copy-start
  70.9 1.9 %copy-done = bf16[2,1024,768]{2,1,0:T(8,128)(2,1)S(1)} copy-done((bf16[2,1024,768]{2,1,0:T(8,128)(2,1)S(1)}, bf16[2,1024,768]{2,1,0:T(8,128)(2,1)}, u32[]{:S(2)}) %copy-start) | copy-done | bytes 3145752
  72.7 0.0 copy-start.1
  72.7 10.4 %visibilities.1 = f32[2,2,1024,1024]{3,2,1,0:T(8,128)} custom-call(bf16[2,1024,768]{2,1,0:T(8,128)(2,1)S(1)} %copy-done), custom_call_target="tpu_custom_call" | custom-call | tf_op jit(solution)/shard_map/visibilities/pallas_call | solution.py:327
  83.1 0.0 copy-done.1
  83.1 0.7 copy.11
Async XLA Ops:
  70.9 1.9 %copy-start = (bf16[2,1024,768]{2,1,0:T(8,128)(2,1)S(1)}, bf16[2,1024,768]{2,1,0:T(8,128)(2,1)}, u32[]{:S(2)}) copy-start(bf16[2,1024,768]{2,1,0:T(8,128)(2,1)} %get-tuple-element.4.x) | copy-start | bytes 9437188
  72.7 10.4 %copy-start.1 = (f32[2,24,1024]{2,1,0:T(8,128)S(1)}, f32[2,24,1024]{2,1,0:T(8,128)}, u32[]{:S(2)}) copy-start(f32[2,24,1024]{2,1,0:T(8,128)} %get-tuple-element.9) | copy-start | bytes 589828

commit v2 on v1

--- a/solution.py
+++ b/solution.py
@@ -66,16 +66,31 @@
     return jnp.transpose(jnp.broadcast_to(row.astype(F32), (128, 128)))
 
 
-def main_kernel(samples, taps, thigh, tlow, antrow, pos, dirs, pointing,
+def main_kernel(samples_hbm, taps_hbm, thigh_hbm, tlow_hbm, antrow_hbm, place_hbm, dirs_hbm, pointing_hbm,
                 xs, beam,
-                eo, stage, send, recv, pos1, pos2, table, weights, perm, lcol, mcol, plain, full,
-                lsem, ssem, rsem, psem, qsem):
+                eo, stage, send, recv, pos1, pos2, table, weights, perm, lcol, mcol, full, pos,
+                samples, taps, thigh, tlow, antrow, place, dirs, pointing,
+                lsem, ssem, rsem, psem, qsem, isem):
+    needed = [0] + [(k * SPC + TAPS - 1) * FRAME for k in range(1, CHUNKS + 1)]
+    slabs = [pltpu.make_async_copy(
+        samples_hbm.at[:, lo:hi], samples.at[:, lo:hi], isem.at[7 + k])
+        for k, (lo, hi) in enumerate(zip(needed[:-1], needed[1:]))]
+    small = [pltpu.make_async_copy(src, dst, isem.at[k]) for k, (src, dst) in enumerate((
+        (place_hbm, place), (taps_hbm, taps), (thigh_hbm, thigh), (tlow_hbm, tlow),
+        (antrow_hbm, antrow), (dirs_hbm, dirs), (pointing_hbm, pointing)))]
+    for copy in small[:2] + slabs[:1] + small[2:] + slabs[1:]:
+        copy.start()
+    small[0].wait()
     r, c = lax.axis_index("row"), lax.axis_index("col")
     me = r * COLS + c
 
     def peer(i):
         k, j = lax.rem(i, COLS), lax.div(i, COLS)
         return lax.rem(r + j + 3 * k, ROWS), lax.rem(c + k, COLS)
+
+    pos[...] = jnp.zeros((1, 128), F32)
+    for xy in range(2):
+        pos[0:1, xy * LOCAL:(xy + 1) * LOCAL] = place[xy:xy + 1, :]
 
     barrier = pltpu.get_barrier_semaphore()
 
@@ -95,6 +110,9 @@
         return pltpu.make_async_copy(send.at[chunk, me], recv.at[chunk, me], lsem.at[chunk])
 
     def channelize(chunk):
+        slabs[chunk].wait()
+        if chunk == 0:
+            small[1].wait()
         def filt(u, carry):
             first = chunk * SPC + 8 * u
             for j in range(2):
@@ -130,6 +148,10 @@
         else:
             lax.fori_loop(0, SPC // 8, filt, 0)
 
+        if chunk == 0:
+            for copy in small[2:4]:
+                copy.wait()
+
         def dft(g, carry):
             for p in range(2):
                 x = jnp.concatenate([
@@ -183,6 +205,8 @@
     channelize(2)
     own(2).start()
 
+    for copy in small[4:]:
+        copy.wait()
     lane = lax.broadcasted_iota(jnp.int32, (128, 128), 1).astype(F32)
     for blk in range(8):
         wanted = column(antrow[blk:blk + 1, :])
@@ -207,12 +231,15 @@
         table[pl.ds(i, 1), :] = pos2[i // ROWS, i % ROWS]
         return carry
     lax.fori_loop(0, DEVICES, spread, 0)
-    rest = table[...]
-    parts = []
-    for _ in range(3):
-        part = rest.astype(BF16)
-        rest = rest - part.astype(F32)
-        parts.append(part)
+
+    def thirds(rest):
+        parts = []
+        for _ in range(3):
+            part = rest.astype(BF16)
+            rest = rest - part.astype(F32)
+            parts.append(part)
+        return parts
+    parts = thirds(table[...])
     picked = []
     antenna = lax.broadcasted_iota(jnp.int32, (128, ANT), 1)
     entry = lax.broadcasted_iota(jnp.int32, (128, ANT), 0)
@@ -221,7 +248,11 @@
         pick = jnp.where(entry == antenna % LOCAL + LOCAL * xy, 1.0, 0.0).astype(BF16)
         whole = sum(lax.dot_general(part, pick, NN, preferred_element_type=F32) for part in parts[::-1])
         picked.append(jnp.sum(jnp.where(mine, whole, 0.0), 0, keepdims=True))
-    xpos, ypos = picked
+    split = [part.astype(F32) for along in picked for part in thirds(along)]
+    split = jnp.concatenate(split + [jnp.zeros((2, ANT), F32)], 0).astype(BF16)
+    moved = lax.dot_general(split, perm[...], NN, preferred_element_type=F32)
+    xpos = (moved[2:3] + moved[1:2]) + moved[0:1]
+    ypos = (moved[5:6] + moved[4:5]) + moved[3:4]
 
     factors = [(2 * me + p + 1).astype(F32) * (1.0 / CHANNELS) for p in range(2)]
 
@@ -251,27 +282,29 @@
         every = pl.ds(0, DEVICES - 1)
         pltpu.make_async_copy(send.at[chunk, every], recv.at[chunk, every], rsem.at[chunk]).wait()
         lanes = pl.ds(pl.multiple_of(chunk * 256, 256), 256)
-
-        def channel(p, carry):
-            def gather(u, carry):
-                z = recv[chunk, pl.ds(u * 16, 16), pl.ds(pl.multiple_of(p * 16, 16), 16), :].astype(F32)
-                rows = pl.ds(pl.multiple_of(u * 128, 128), 128)
-                plain[rows, 0:128] = z[:, 0:8, :].reshape(128, 128).astype(BF16)
-                plain[rows, 128:256] = z[:, 8:16, :].reshape(128, 128).astype(BF16)
-                return carry
-            lax.fori_loop(0, 8, gather, 0)
-            x = lax.dot_general(perm[...], plain[...], NN, preferred_element_type=F32)
-            xb = x.astype(BF16)
-            full[0:ANT, :] = xb
-            xs[p, :, lanes] = xb
-            full[ANT:2 * ANT, 0:128] = x[:, 128:256].astype(BF16)
-            full[ANT:2 * ANT, 128:256] = (-x[:, 0:128]).astype(BF16)
-            v = lax.dot_general(weights[p], full[...], NN, preferred_element_type=F32)
+        bins_at = pl.ds(pl.multiple_of(chunk * 8, 8), 8)
+
+        def gather(u, carry):
+            rows = pl.ds(pl.multiple_of(u * 128, 128), 128)
+            below = pl.ds(pl.multiple_of(ANT + u * 128, 128), 128)
+            z = recv[chunk, pl.ds(u * 16, 16)].astype(F32)
+            for p in range(2):
+                re = z[:, p * 16:p * 16 + 8, :].reshape(128, 128)
+                im = z[:, p * 16 + 8:p * 16 + 16, :].reshape(128, 128)
+                full[p, rows, 0:128] = re.astype(BF16)
+                full[p, rows, 128:256] = im.astype(BF16)
+                full[p, below, 0:128] = im.astype(BF16)
+                full[p, below, 128:256] = (-re).astype(BF16)
+            return carry
+        lax.fori_loop(0, 8, gather, 0)
+        for p in range(2):
+            v = lax.dot_general(weights[p], full[p], NN, preferred_element_type=F32)
             power = v[:, 0:128] * v[:, 0:128] + v[:, 128:256] * v[:, 128:256]
             bins = jnp.sum(jnp.transpose(power).reshape(SPC // INTEG, INTEG, BEAMS), axis=1)
-            beam[p, pl.ds(pl.multiple_of(chunk * 8, 8), 8), :] = bins
-            return carry
-        return lax.fori_loop(0, 2, channel, carry)
+            beam[p, bins_at, :] = bins
+            x = lax.dot_general(perm[...], full[p, 0:ANT, :], NN, preferred_element_type=F32)
+            xs[p, :, lanes] = x.astype(BF16)
+        return carry
     lax.fori_loop(0, CHUNKS, beams, 0)
 
     for chunk in range(CHUNKS):
@@ -279,25 +312,38 @@
         pltpu.make_async_copy(send.at[chunk, every], recv.at[chunk, every], ssem.at[chunk]).wait()
 
 
-def gram_kernel(x, out):
+def gram_kernel(x, out, kept):
     u = pl.program_id(1)
-    right = x[0, pl.ds(pl.multiple_of(u * 256, 256), 256), :]
     scale = 1.0 / SPECTRA
-    out[0, 0] = lax.dot_general(x[0], right, NT, preferred_element_type=F32) * scale
-    turned = jnp.concatenate(
-        [piece for k in range(CHUNKS) for piece in (-right[:, k * 256 + 128:(k + 1) * 256], right[:, k * 256:k * 256 + 128])], 1)
-    out[0, 1] = lax.dot_general(x[0], turned, NT, preferred_element_type=F32) * scale
+
+    def panel(b):
+        lo, hi = b * 256, (b + 1) * 256
+        right = x[0, lo:hi, :]
+        turned = jnp.concatenate(
+            [piece for k in range(CHUNKS) for piece in (-right[:, k * 256 + 128:(k + 1) * 256], right[:, k * 256:k * 256 + 128])], 1)
+        for q, other in enumerate((right, turned)):
+            col = lax.dot_general(x[0, lo:, :], other, NT, preferred_element_type=F32) * scale
+            out[0, q, :, lo:hi] = col[0:256]
+            if hi < ANT:
+                kept[q, hi:, lo:hi] = col[256:]
+            for j in range(b + 1, ANT // 256):
+                flip = jnp.transpose(col[(j - b) * 256:(j - b + 1) * 256])
+                out[0, q, :, j * 256:(j + 1) * 256] = -flip if q else flip
+            if lo > 0:
+                out[0, q, :, 0:lo] = kept[q, lo:hi, 0:lo]
+
+    for b in range(ANT // 256):
+        pl.when(u == b)(functools.partial(panel, b))
 
 
 def body(samples, pfb_taps, antenna_input_row, positions, directions, pointing):
     high, low = dft_tables()
-    pos = jnp.pad(positions.reshape(1, 2 * LOCAL), ((0, 0), (0, 128 - 2 * LOCAL)))
     vmem = pl.BlockSpec(memory_space=pltpu.VMEM)
     xs, beam = pl.pallas_call(
         main_kernel,
         out_shape=(jax.ShapeDtypeStruct((2, ANT, 2 * SPECTRA), BF16),
                    jax.ShapeDtypeStruct((2, SPECTRA // INTEG, BEAMS), F32)),
-        in_specs=[vmem] * 8,
+        in_specs=[pl.BlockSpec(memory_space=pltpu.MemorySpace.HBM)] * 8,
         out_specs=(vmem, vmem),
         scratch_shapes=[
             pltpu.VMEM((4, LOCAL * PITCH, 128), F32),
@@ -311,26 +357,36 @@
             pltpu.VMEM((ANT, ANT), BF16),
             pltpu.VMEM((BEAMS, 128), F32),
             pltpu.VMEM((BEAMS, 128), F32),
-            pltpu.VMEM((ANT, 256), BF16),
-            pltpu.VMEM((2 * ANT, 256), BF16),
+            pltpu.VMEM((2, 2 * ANT, 256), BF16),
+            pltpu.VMEM((1, 128), F32),
+            pltpu.VMEM((LOCAL, (SPECTRA + TAPS - 1) * FRAME), BF16),
+            pltpu.VMEM((TAPS, FRAME), F32),
+            pltpu.VMEM((2, HALF, HALF), BF16),
+            pltpu.VMEM((2, HALF, HALF), BF16),
+            pltpu.VMEM((8, 128), jnp.int32),
+            pltpu.VMEM((2, LOCAL), F32),
+            pltpu.VMEM((2, ANT), F32),
+            pltpu.VMEM((8, 128), jnp.int32),
             pltpu.SemaphoreType.DMA((4,)),
             pltpu.SemaphoreType.DMA((CHUNKS,)),
             pltpu.SemaphoreType.DMA((CHUNKS,)),
             pltpu.SemaphoreType.DMA((2,)),
             pltpu.SemaphoreType.DMA((2,)),
+            pltpu.SemaphoreType.DMA((7 + CHUNKS,)),
         ],
         compiler_params=pltpu.CompilerParams(
-            collective_id=0, has_side_effects=True, vmem_limit_bytes=60 * 1024 * 1024),
+            collective_id=0, has_side_effects=True, vmem_limit_bytes=63 * 1024 * 1024),
         name="channelize_exchange_beams",
-    )(samples, pfb_taps, jnp.asarray(high), jnp.asarray(low), antenna_input_row.reshape(8, 128), pos,
+    )(samples, pfb_taps, jnp.asarray(high), jnp.asarray(low), antenna_input_row.reshape(8, 128), positions,
       directions, pointing.reshape(8, 128))
     vis = pl.pallas_call(
         gram_kernel,
         grid=(2, 4),
         out_shape=jax.ShapeDtypeStruct((2, 2, ANT, ANT), F32),
         in_specs=[pl.BlockSpec((1, ANT, 2 * SPECTRA), lambda p, u: (p, 0, 0))],
-        out_specs=pl.BlockSpec((1, 2, ANT, 256), lambda p, u: (p, 0, 0, u)),
-        compiler_params=pltpu.CompilerParams(vmem_limit_bytes=40 * 1024 * 1024),
+        out_specs=pl.BlockSpec((1, 2, 256, ANT), lambda p, u: (p, 0, u, 0)),
+        scratch_shapes=[pltpu.VMEM((2, ANT, ANT), F32)],
+        compiler_params=pltpu.CompilerParams(vmem_limit_bytes=63 * 1024 * 1024),
         name="visibilities",
     )(xs)
     return vis, beam

time: 85.2 us -> 76.3 us (0.90); the launches traced: 83.8 us -> 76.1 us
  Pallas kernels: 79.3 us -> 74.8 us
  local copies, waits for them, and re-layouts: 3.84 us -> 0.68 us
    pallas_call x1, Pallas kernels: 68.9 us -> 61.6 us  [body(): pl.pallas_call(main_kernel, out_shape=(jax.ShapeDtypeStruct((2, ANT, 2 *...]
    pallas_call x1, Pallas kernels: 10.4 us -> 13.1 us  [body(): pl.pallas_call(gram_kernel, grid=(2, 4), out_shape=jax.ShapeDtypeStruct((...]
    unnamed x5 -> x3, local copies, waits for them, and re-layouts: 2.56 us -> 0.68 us
where the time goes in v2:
time: 76.3 us; the launch traced here: 76.1 us
  Pallas kernels  74.8 us (98%)
    pallas_call x1, Pallas kernels, body(): pl.pallas_call(main_kernel, out_shape=(jax.ShapeDtypeStruct((2, ANT, 2 *...  61.6 us
    pallas_call x1, Pallas kernels, body(): pl.pallas_call(gram_kernel, grid=(2, 4), out_shape=jax.ShapeDtypeStruct((...  13.1 us

profile of v2, /device:TPU:57, one launch (start us, length us, event | category | flops | bytes accessed | tf_op | source)
XLA Modules:
  0.0 76.1 jit_solution(12593048540151333257)
XLA Ops:
  0.6 61.6 %channelize_exchange_beams.1 = (bf16[2,1024,768]{2,1,0:T(8,128)(2,1)}, f32[2,24,1024]{2,1,0:T(8,128)}) custom-call(bf16[8,200192]{1,0:T(8,128)(2,1)} %samples_hbm.1, f32[8,512]{1,0:T(8,128)} %taps_hbm.1, bf16[2,256,256]{2,1,0:T(8,128)(2,1)} %constant.4.clone.thigh_hbm, bf16[2,256,256]{2,1,0:T(8,128)(2,1)} %constant.5.clone.tlow_hbm, s32[8,128]{1,0:T(8,128)} %bitcast.2, ...), custom_call_target="tpu_custom_call" | custom-call | tf_op jit(solution)/shard_map/channelize_exchange_beams/pallas_call | solution.py:342
  62.3 0.0 copy-start
  62.3 13.1 %visibilities.1 = f32[2,2,1024,1024]{3,2,1,0:T(8,128)} custom-call(bf16[2,1024,768]{2,1,0:T(8,128)(2,1)} %get-tuple-element.4.x), custom_call_target="tpu_custom_call" | custom-call | tf_op jit(solution)/shard_map/visibilities/pallas_call | solution.py:382
  75.4 0.0 copy-done
  75.4 0.7 copy.11
Async XLA Ops:
  62.3 13.2 %copy-start = (f32[2,24,1024]{2,1,0:T(8,128)S(1)}, f32[2,24,1024]{2,1,0:T(8,128)}, u32[]{:S(2)}) copy-start(f32[2,24,1024]{2,1,0:T(8,128)} %get-tuple-element.9) | copy-start | bytes 589828

commit v3 on v2

--- a/solution.py
+++ b/solution.py
@@ -312,17 +312,29 @@
         pltpu.make_async_copy(send.at[chunk, every], recv.at[chunk, every], ssem.at[chunk]).wait()
 
 
-def gram_kernel(x, out, kept):
-    u = pl.program_id(1)
+def gram_kernel(x_hbm, out, kept, x, sem):
+    p, u = pl.program_id(0), pl.program_id(1)
+    fetches = [pltpu.make_async_copy(x_hbm.at[k], x.at[k], sem.at[k]) for k in range(2)]
+
+    @pl.when((p == 0) & (u == 0))
+    def _():
+        fetches[0].start()
+        fetches[1].start()
+        fetches[0].wait()
+
+    @pl.when((p == 1) & (u == 0))
+    def _():
+        fetches[1].wait()
+
     scale = 1.0 / SPECTRA
 
     def panel(b):
         lo, hi = b * 256, (b + 1) * 256
-        right = x[0, lo:hi, :]
+        right = x[p, lo:hi, :]
         turned = jnp.concatenate(
             [piece for k in range(CHUNKS) for piece in (-right[:, k * 256 + 128:(k + 1) * 256], right[:, k * 256:k * 256 + 128])], 1)
         for q, other in enumerate((right, turned)):
-            col = lax.dot_general(x[0, lo:, :], other, NT, preferred_element_type=F32) * scale
+            col = lax.dot_general(x[p, lo:, :], other, NT, preferred_element_type=F32) * scale
             out[0, q, :, lo:hi] = col[0:256]
             if hi < ANT:
                 kept[q, hi:, lo:hi] = col[256:]
@@ -383,9 +395,10 @@
         gram_kernel,
         grid=(2, 4),
         out_shape=jax.ShapeDtypeStruct((2, 2, ANT, ANT), F32),
-        in_specs=[pl.BlockSpec((1, ANT, 2 * SPECTRA), lambda p, u: (p, 0, 0))],
+        in_specs=[pl.BlockSpec(memory_space=pl.ANY)],
         out_specs=pl.BlockSpec((1, 2, 256, ANT), lambda p, u: (p, 0, u, 0)),
-        scratch_shapes=[pltpu.VMEM((2, ANT, ANT), F32)],
+        scratch_shapes=[pltpu.VMEM((2, ANT, ANT), F32), pltpu.VMEM((2, ANT, 2 * SPECTRA), BF16),
+                        pltpu.SemaphoreType.DMA((2,))],
         compiler_params=pltpu.CompilerParams(vmem_limit_bytes=63 * 1024 * 1024),
         name="visibilities",
     )(xs)

time: 76.3 us -> 74.8 us (0.980)
  Pallas kernels: 74.8 us -> 73.3 us
    pallas_call x1, Pallas kernels: 13.1 us -> 11.7 us  [body(): pl.pallas_call(gram_kernel, grid=(2, 4), out_shape=jax.ShapeDtypeStruct((...]
where the time goes in v3:
time: 74.8 us; the launch traced here: 74.6 us
  Pallas kernels  73.3 us (98%)
    pallas_call x1, Pallas kernels, body(): pl.pallas_call(main_kernel, out_shape=(jax.ShapeDtypeStruct((2, ANT, 2 *...  61.6 us
    pallas_call x1, Pallas kernels, body(): pl.pallas_call(gram_kernel, grid=(2, 4), out_shape=jax.ShapeDtypeStruct((...  11.7 us

profile of v3, /device:TPU:57, one launch (start us, length us, event | category | flops | bytes accessed | tf_op | source)
XLA Modules:
  0.0 74.6 jit_solution(1812429647677059132)
XLA Ops:
  0.6 61.6 %channelize_exchange_beams.1 = (bf16[2,1024,768]{2,1,0:T(8,128)(2,1)}, f32[2,24,1024]{2,1,0:T(8,128)}) custom-call(bf16[8,200192]{1,0:T(8,128)(2,1)} %samples_hbm.1, f32[8,512]{1,0:T(8,128)} %taps_hbm.1, bf16[2,256,256]{2,1,0:T(8,128)(2,1)} %constant.4.clone.thigh_hbm, bf16[2,256,256]{2,1,0:T(8,128)(2,1)} %constant.5.clone.tlow_hbm, s32[8,128]{1,0:T(8,128)} %bitcast.2, ...), custom_call_target="tpu_custom_call" | custom-call | tf_op jit(solution)/shard_map/channelize_exchange_beams/pallas_call | solution.py:354
  62.3 0.0 copy-start
  62.3 11.7 %visibilities.1 = f32[2,2,1024,1024]{3,2,1,0:T(8,128)} custom-call(bf16[2,1024,768]{2,1,0:T(8,128)(2,1)} %get-tuple-element.4.x_hbm), custom_call_target="tpu_custom_call" | custom-call | tf_op jit(solution)/shard_map/visibilities/pallas_call | solution.py:394
  74.0 0.0 copy-done
  74.0 0.7 copy.11
Async XLA Ops:
  62.3 11.7 %copy-start = (f32[2,24,1024]{2,1,0:T(8,128)S(1)}, f32[2,24,1024]{2,1,0:T(8,128)}, u32[]{:S(2)}) copy-start(f32[2,24,1024]{2,1,0:T(8,128)} %get-tuple-element.9) | copy-start | bytes 589828
